TPU v7x, 256 devices: a whole 4x4x8 slice. The times are simulated.
256 devices in a mesh: row: 8 (over y, z_lo), col: 32 (over x, z_hi, core).
Axes of the slice: x: 4, y: 4, z: 8 (z_hi: 4, z_lo: 2; z = z_hi * 2 + z_lo), core: 2. Of those that a mesh axis runs over, the one named last changes fastest.
Arguments:
- features: bfloat16 [32768, 128], P(('col', 'row')), may hold values from -6 to 6
- weight: bfloat16 [128, 256], replicated, may hold values from -0.5 to 0.5
- history: bfloat16 [32768, 256], P(('col', 'row')), may hold values from -6 to 6
- in_batch: int32 [32768], P(('col', 'row')), may hold values 0 or 1
- tile_values: bfloat16 [8, 32, 192, 128, 128], P('row', 'col'), as said below
- tile_pos: int32 [8, 32, 192, 2], P('row', 'col'), may hold values from 0 to 31, as said below
- tile_count: int32 [8, 32], P('row', 'col'), may hold values from 1 to 192, as said below
- cotangent: bfloat16 [32768, 256], P(('row', 'col')), may hold values from -6 to 6
Outputs:
- output: bfloat16 [32768, 256], P(('row', 'col'))
- grad_features: bfloat16 [32768, 128], P(('col', 'row'))
- grad_weight: float32 [128, 256], replicated
Inputs may be any that keep to these rules, and one draw needn't show every extreme that they name: tile_pos[..., 0] lies in 0 to 128 * 32 / 128 - 1 and tile_pos[..., 1] in 0 to 128 * 8 / 128 - 1. `tile_count`: at least one block uses all 192 slots. `tile_values`: entries are nonnegative.
All inputs are finite; a program needn't handle non-finite values. No bound on the sum of `in_batch` on one device may be relied on, other than what follows from the above.
Results may differ from a plain program's by a relative error of at most 0.006.
Values may be sent and summed in bfloat16 or wider, within the bound.
No kernel may reach another device: no remote copies, remote signals or barrier semaphores. Data moves between devices by JAX's collectives and lax.ppermute only.
A program may use at most 128 MiB of HBM per device.

v0:
```python
import math
import jax
import jax.numpy as jnp
from jax import lax
from jax.sharding import PartitionSpec as P


def gelu_form(values):
    return jax.nn.gelu(values, approximate=True)


def tile_sweep(group_step, start_value, tiles, coords, valid):
    total_slots = tiles.shape[0]
    group = math.gcd(total_slots, 64)
    tiles_grouped = tiles.reshape(total_slots // group, group, tiles.shape[1], tiles.shape[2])
    coords_grouped = coords.reshape(total_slots // group, group, 2)
    valid_grouped = valid.reshape(total_slots // group, group)

    def scan_step(running, pieces):
        return (group_step(running, pieces[0], pieces[1], pieces[2]), None)

    result, _ = lax.scan(scan_step, start_value, (tiles_grouped, coords_grouped, valid_grouped))
    return result


def body(features, weight, history, in_batch, tile_values, tile_pos, tile_count, cotangent):
    node_count = features.shape[0]
    width = weight.shape[1]
    rows_size = lax.axis_size("row")
    cols_size = lax.axis_size("col")
    block_rows = node_count * cols_size
    block_cols = node_count * rows_size
    tiles = tile_values.reshape(tile_values.shape[2], tile_values.shape[3], tile_values.shape[4])
    coords = tile_pos.reshape(tile_pos.shape[2], 2)
    count = tile_count.reshape(())
    valid = (jnp.arange(tiles.shape[0], dtype=jnp.int32) < count).astype(jnp.float32)
    projected = jnp.dot(features, weight, preferred_element_type=jnp.float32).astype(jnp.bfloat16)
    mixed = jnp.where(in_batch[:, None] == 1, projected, history)
    panel = lax.all_gather(mixed, "row", axis=0, tiled=True)
    panel_tiles = panel.reshape(block_cols // 128, 128, width)

    def forward_group(running, tiles_part, coords_part, valid_part):
        picked = panel_tiles[coords_part[:, 1]]
        product = jnp.einsum("tij,tjh->tih", tiles_part, picked, preferred_element_type=jnp.float32)
        product = product * valid_part[:, None, None]
        return running + jax.ops.segment_sum(
            product, coords_part[:, 0], num_segments=block_rows // 128
        )

    forward_start = jnp.zeros((block_rows // 128, 128, width), jnp.float32)
    partial_rows = tile_sweep(forward_group, forward_start, tiles, coords, valid).reshape(
        block_rows, width
    )
    total = lax.psum_scatter(partial_rows, "col", scatter_dimension=0, tiled=True)
    output = gelu_form(total).astype(jnp.bfloat16)
    _, pullback = jax.vjp(gelu_form, total)
    grad_total = pullback(cotangent.astype(jnp.float32))[0].astype(jnp.bfloat16)
    grad_rows = lax.all_gather(grad_total, "col", axis=0, tiled=True)
    grad_tiles = grad_rows.reshape(block_rows // 128, 128, width)

    def backward_group(running, tiles_part, coords_part, valid_part):
        picked = grad_tiles[coords_part[:, 0]]
        product = jnp.einsum("tij,tih->tjh", tiles_part, picked, preferred_element_type=jnp.float32)
        product = product * valid_part[:, None, None]
        return running + jax.ops.segment_sum(
            product, coords_part[:, 1], num_segments=block_cols // 128
        )

    backward_start = jnp.zeros((block_cols // 128, 128, width), jnp.float32)
    partial_cols = tile_sweep(backward_group, backward_start, tiles, coords, valid).reshape(
        block_cols, width
    )
    grad_mixed = lax.psum_scatter(partial_cols, "row", scatter_dimension=0, tiled=True)
    grad_projected = (grad_mixed * in_batch[:, None].astype(jnp.float32)).astype(jnp.bfloat16)
    grad_features = jnp.dot(grad_projected, weight.T, preferred_element_type=jnp.float32).astype(
        jnp.bfloat16
    )
    weight_term = jnp.dot(features.T, grad_projected, preferred_element_type=jnp.float32)
    weight_total = lax.psum(weight_term, ("row", "col"))
    scale_factor = 1.0 / math.sqrt(node_count * rows_size * cols_size)
    grad_weight = weight_total * jnp.float32(scale_factor)
    return (output, grad_features, grad_weight)


def solution(mesh):
    in_specs = (
        P(("col", "row"), None),
        P(),
        P(("col", "row"), None),
        P(("col", "row")),
        P("row", "col", None, None, None),
        P("row", "col", None, None),
        P("row", "col"),
        P(("row", "col"), None),
    )
    out_specs = (P(("row", "col"), None), P(("col", "row"), None), P())
    return jax.shard_map(body, mesh=mesh, in_specs=in_specs, out_specs=out_specs, check_vma=False)
```

profile of v0, /device:TPU:2, one launch (start us, length us, event | category | flops | bytes accessed | tf_op | source)
XLA Modules:
  0.0 661.4 jit_solution(3899024853442598339)
XLA Ops:
  7.2 0.0 copy-start
  7.2 0.0 reduce-scatter.3.cloned.1.call-start
  7.2 0.8 reshape_reshape.8
  8.7 0.7 broadcast_compare_fusion
  9.3 1.0 fusion.10
  10.3 30.2 %all_gather.6 = bf16[1024,256]{1,0:T(8,128)(2,1)S(1)} all-gather(bf16[128,256]{1,0:T(8,128)(2,1)S(1)} %fusion.10), channel_id=1, replica_groups=mesh['row'=8,'col'=32] {'row'}, dimensions={0}, use_global_device_ids=true | all-gather | bytes 589824 | tf_op jit(solution)/shard_map/all_gather | solution.py:39
  40.5 2.4 broadcast.43
  42.9 87.8 %while.20 = (s32[]{:T(128)}, f32[32,128,256]{2,1,0:T(8,128)}, s32[3,64,2]{1,2,0:T(2,128)S(1)}, bf16[3,64,128,128]{3,2,1,0:T(8,128)(2,1)}, bf16[8,128,256]{2,1,0:...) while((s32[]{:T(128)}, f32[32,128,256]{2,1,0:T(8,128)}, s32[3,64,2]{1,2,0:T(2,128)S(1)}, ...), condition=%wide.region_2.3_spmd, body=%wide.region_0.2_spmd.sunk | while | flops 541066432 | bytes 48242772 | solution.py:22
  43.0 2.8 gather_fusion
  45.7 7.3 %broadcast_multiply_fusion.5 = f32[64,128,256]{2,1,0:T(8,128)} fusion(f32[64]{0:T(128)S(1)} %fusion.39, bf16[64,128,256]{2,1,0:T(8,128)(2,1)} %gather_fusion, bf16[3,64,128,128]{3,2,1,0:T(8,128)(2,1)} %get-tuple-element.222, s32[]{:T(128)} %get-tuple-element.212), kind=kOutput, calls=%fused_computation.4.clone.1 | convolution fusion | flops 538968064 | bytes 14680832 | tf_op jit(solution)/shard_map/while/body/eval_jaxpr/tij,tjh->tih/dot_general | solution.py:44
  53.0 19.1 %scatter_fusion = f32[32,128,256]{2,1,0:T(8,128)} fusion(f32[32,128,256]{2,1,0:T(8,128)} %get-tuple-element.213, s32[64]{0:T(128)S(1)} %get-tuple-element.195, f32[64,128,256]{2,1,0:T(8,128)} %broadcast_multiply_fusion.5), kind=kCustom, calls=%fused_computation.2.clone.1 | custom fusion | flops 2097152 | bytes 25166080 | tf_op jit(solution)/shard_map/while/body/eval_jaxpr/scatter-add | solution.py:46
  72.2 2.8 gather_fusion
  75.0 7.3 %broadcast_multiply_fusion.5 = f32[64,128,256]{2,1,0:T(8,128)} fusion(f32[64]{0:T(128)S(1)} %fusion.39, bf16[64,128,256]{2,1,0:T(8,128)(2,1)} %gather_fusion, bf16[3,64,128,128]{3,2,1,0:T(8,128)(2,1)} %get-tuple-element.222, s32[]{:T(128)} %get-tuple-element.212), kind=kOutput, calls=%fused_computation.4.clone.1 | convolution fusion | flops 538968064 | bytes 14680832 | tf_op jit(solution)/shard_map/while/body/eval_jaxpr/tij,tjh->tih/dot_general | solution.py:44
  82.3 19.3 %scatter_fusion = f32[32,128,256]{2,1,0:T(8,128)} fusion(f32[32,128,256]{2,1,0:T(8,128)} %get-tuple-element.213, s32[64]{0:T(128)S(1)} %get-tuple-element.195, f32[64,128,256]{2,1,0:T(8,128)} %broadcast_multiply_fusion.5), kind=kCustom, calls=%fused_computation.2.clone.1 | custom fusion | flops 2097152 | bytes 25166080 | tf_op jit(solution)/shard_map/while/body/eval_jaxpr/scatter-add | solution.py:46
  101.6 2.8 gather_fusion
  104.3 7.3 %broadcast_multiply_fusion.5 = f32[64,128,256]{2,1,0:T(8,128)} fusion(f32[64]{0:T(128)S(1)} %fusion.39, bf16[64,128,256]{2,1,0:T(8,128)(2,1)} %gather_fusion, bf16[3,64,128,128]{3,2,1,0:T(8,128)(2,1)} %get-tuple-element.222, s32[]{:T(128)} %get-tuple-element.212), kind=kOutput, calls=%fused_computation.4.clone.1 | convolution fusion | flops 538968064 | bytes 14680832 | tf_op jit(solution)/shard_map/while/body/eval_jaxpr/tij,tjh->tih/dot_general | solution.py:44
  111.6 19.1 %scatter_fusion = f32[32,128,256]{2,1,0:T(8,128)} fusion(f32[32,128,256]{2,1,0:T(8,128)} %get-tuple-element.213, s32[64]{0:T(128)S(1)} %get-tuple-element.195, f32[64,128,256]{2,1,0:T(8,128)} %broadcast_multiply_fusion.5), kind=kCustom, calls=%fused_computation.2.clone.1 | custom fusion | flops 2097152 | bytes 25166080 | tf_op jit(solution)/shard_map/while/body/eval_jaxpr/scatter-add | solution.py:46
  130.8 0.0 reduce-scatter.3.cloned.1.call-update
  130.8 0.0 all-gather.2.cloned.1.call-start
  130.9 101.0 %reduce-scatter.3.cloned.1.call-done = f32[128,256]{1,0:T(8,128)} async-done(((f32[4096,256]{1,0:T(8,128)}), f32[128,256]{1,0:T(8,128)}) %reduce-scatter.3.cloned.1.call-update) | async-done | bytes 131088 | tf_op jit(solution)/shard_map/reduce_scatter | solution.py:54
  231.8 1.7 fusion.13
  233.5 0.0 all-gather.2.cloned.1.call-update
  233.5 0.0 reduce-scatter.5.cloned.1.call-start
  233.6 8.6 %copy.14 = bf16[1,1,192,128,128]{3,4,2,1,0:T(8,128)(2,1)} copy(bf16[1,1,192,128,128]{4,3,2,1,0:T(8,128)(2,1)} %bitcast.65) | data formatting | bytes 12582912 | tf_op args[4]
  242.1 45.0 %all-gather.2.cloned.1.call-done = bf16[4096,256]{1,0:T(8,128)(2,1)} async-done(((bf16[128,256]{1,0:T(8,128)(2,1)}), bf16[4096,256]{1,0:T(8,128)(2,1)}) %all-gather.2.cloned.1.call-update) | async-done | bytes 2097168 | tf_op jit(solution)/shard_map/all_gather | solution.py:58
  287.2 0.1 broadcast.48
  287.3 0.0 copy-start.4
  287.3 0.0 copy-start.2
  287.3 72.3 %while.21 = (s32[]{:T(128)}, f32[8,128,256]{2,1,0:T(8,128)S(1)}, s32[3,64,2]{1,2,0:T(2,128)S(1)}, bf16[3,64,128,128]{2,3,1,0:T(8,128)(2,1)}, bf16[32,128,256]{2,...) while((s32[]{:T(128)}, f32[8,128,256]{2,1,0:T(8,128)S(1)}, s32[3,64,2]{1,2,0:T(2,128)S(1)}, ...), condition=%wide.region_6.7_spmd, body=%wide.region_4.6_spmd.sunk | while | flops 541066432 | bytes 48242772 | solution.py:22
  287.3 4.4 gather_fusion.1
  291.7 7.3 %broadcast_multiply_fusion.6 = f32[64,128,256]{2,1,0:T(8,128)} fusion(f32[64]{0:T(128)S(1)} %fusion.43, bf16[64,128,256]{2,1,0:T(8,128)(2,1)} %gather_fusion.1, bf16[3,64,128,128]{2,3,1,0:T(8,128)(2,1)} %get-tuple-element.243, s32[]{:T(128)} %get-tuple-element.233), kind=kOutput, calls=%fused_computation.15.clone.1 | convolution fusion | flops 538968064 | bytes 14680832 | tf_op jit(solution)/shard_map/while/body/eval_jaxpr/tij,tih->tjh/dot_general | solution.py:63
  299.0 12.4 %scatter_fusion.1 = f32[8,128,256]{2,1,0:T(8,128)S(1)} fusion(f32[8,128,256]{2,1,0:T(8,128)S(1)} %get-tuple-element.234, s32[64]{0:T(128)S(1)} %get-tuple-element.203, f32[64,128,256]{2,1,0:T(8,128)} %broadcast_multiply_fusion.6), kind=kCustom, calls=%fused_computation.3.clone.1 | custom fusion | flops 2097152 | bytes 25166080 | tf_op jit(solution)/shard_map/while/body/eval_jaxpr/scatter-add | solution.py:65
  311.5 4.4 gather_fusion.1
  315.8 7.3 %broadcast_multiply_fusion.6 = f32[64,128,256]{2,1,0:T(8,128)} fusion(f32[64]{0:T(128)S(1)} %fusion.43, bf16[64,128,256]{2,1,0:T(8,128)(2,1)} %gather_fusion.1, bf16[3,64,128,128]{2,3,1,0:T(8,128)(2,1)} %get-tuple-element.243, s32[]{:T(128)} %get-tuple-element.233), kind=kOutput, calls=%fused_computation.15.clone.1 | convolution fusion | flops 538968064 | bytes 14680832 | tf_op jit(solution)/shard_map/while/body/eval_jaxpr/tij,tih->tjh/dot_general | solution.py:63
  323.1 12.4 %scatter_fusion.1 = f32[8,128,256]{2,1,0:T(8,128)S(1)} fusion(f32[8,128,256]{2,1,0:T(8,128)S(1)} %get-tuple-element.234, s32[64]{0:T(128)S(1)} %get-tuple-element.203, f32[64,128,256]{2,1,0:T(8,128)} %broadcast_multiply_fusion.6), kind=kCustom, calls=%fused_computation.3.clone.1 | custom fusion | flops 2097152 | bytes 25166080 | tf_op jit(solution)/shard_map/while/body/eval_jaxpr/scatter-add | solution.py:65
  335.6 4.4 gather_fusion.1
  339.9 7.3 %broadcast_multiply_fusion.6 = f32[64,128,256]{2,1,0:T(8,128)} fusion(f32[64]{0:T(128)S(1)} %fusion.43, bf16[64,128,256]{2,1,0:T(8,128)(2,1)} %gather_fusion.1, bf16[3,64,128,128]{2,3,1,0:T(8,128)(2,1)} %get-tuple-element.243, s32[]{:T(128)} %get-tuple-element.233), kind=kOutput, calls=%fused_computation.15.clone.1 | convolution fusion | flops 538968064 | bytes 14680832 | tf_op jit(solution)/shard_map/while/body/eval_jaxpr/tij,tih->tjh/dot_general | solution.py:63
  347.2 12.4 %scatter_fusion.1 = f32[8,128,256]{2,1,0:T(8,128)S(1)} fusion(f32[8,128,256]{2,1,0:T(8,128)S(1)} %get-tuple-element.234, s32[64]{0:T(128)S(1)} %get-tuple-element.203, f32[64,128,256]{2,1,0:T(8,128)} %broadcast_multiply_fusion.6), kind=kCustom, calls=%fused_computation.3.clone.1 | custom fusion | flops 2097152 | bytes 25166080 | tf_op jit(solution)/shard_map/while/body/eval_jaxpr/scatter-add | solution.py:65
  359.6 1.0 copy-done.1
  360.6 0.0 reduce-scatter.5.cloned.1.call-update
  360.6 0.0 all-reduce.2.cloned.1.call-start
  360.7 42.6 %reduce-scatter.5.cloned.1.call-done = f32[128,256]{1,0:T(8,128)} async-done(((f32[1024,256]{1,0:T(8,128)}), f32[128,256]{1,0:T(8,128)}) %reduce-scatter.5.cloned.1.call-update) | async-done | bytes 131088 | tf_op jit(solution)/shard_map/reduce_scatter | solution.py:73
  403.3 1.8 convolution_bitcast_fusion
  405.1 0.0 all-reduce.2.cloned.1.call-update
  405.1 1.7 convolution_convert_fusion.1
  406.9 246.3 %all-reduce.2.cloned.1.call-done = f32[128,256]{0,1:T(8,128)} async-done(((f32[128,256]{0,1:T(8,128)}), f32[128,256]{0,1:T(8,128)}) %all-reduce.2.cloned.1.call-update) | async-done | bytes 131088 | tf_op jit(solution)/shard_map/psum | solution.py:79
  653.2 0.9 broadcast_multiply_fusion.2
  654.1 0.8 copy.18
  (33 shorter events, 0.2 us)
Async XLA Ops:
  7.2 2.2 copy-start
  7.2 224.6 %reduce-scatter.3.cloned.1.call-start = ((), (), s32[]{:S(2)}) async-start(), calls=%async_computation.2 | async-start | bytes 4325376 | tf_op jit(solution)/shard_map/reduce_scatter | solution.py:54
  130.8 101.0 %copy-start.3 = (bf16[128,256]{1,0:T(8,128)(2,1)S(1)}, bf16[128,256]{1,0:T(8,128)(2,1)}, u32[]{:S(2)}) copy-start(bf16[128,256]{1,0:T(8,128)(2,1)} %param.19) | copy-start | bytes 196612
  130.8 156.4 %all-gather.2.cloned.1.call-start = ((), (), s32[]{:S(2)}) async-start(), calls=%async_computation.3 | async-start | bytes 2162688 | tf_op jit(solution)/shard_map/all_gather | solution.py:58
  233.5 169.8 %reduce-scatter.5.cloned.1.call-start = ((), (), s32[]{:S(2)}) async-start(), calls=%async_computation.4 | async-start | bytes 1179648 | tf_op jit(solution)/shard_map/reduce_scatter | solution.py:73
  287.3 73.4 %copy-start.4 = (s32[128]{0:T(128)S(1)}, s32[128]{0:T(128)}, u32[]{:S(2)}) copy-start(s32[128]{0:T(128)} %param.15) | copy-start | bytes 1540
  287.3 116.0 %copy-start.2 = (bf16[128,128]{1,0:T(8,128)(2,1)S(1)}, bf16[128,128]{1,0:T(8,128)(2,1)}, u32[]{:S(2)}) copy-start(bf16[128,128]{1,0:T(8,128)(2,1)} %param.12) | copy-start | bytes 98308
  359.6 1.0 copy-start.1
  360.6 292.6 %all-reduce.2.cloned.1.call-start = ((), (), s32[]{:S(2)}) async-start(), calls=%async_computation.5 | async-start | bytes 262144 | tf_op jit(solution)/shard_map/psum | solution.py:79
Sparse Core Ops, SparseCore 0:
  130.9 100.8 reduce-scatter.2
  235.0 52.1 all-gather.1
  360.7 42.4 reduce-scatter.4
  409.2 243.9 all-reduce.1
where the time goes:
time: 662 us; the launch traced here: 661 us
  waiting for transfers between devices  435 us (66%)
  other arithmetic  98 us (15%)
  matrix products  48.4 us (7%)
  local copies, waits for them, and re-layouts  35.1 us (5%)
  blocking collectives  30.2 us (5%)
  between operations  14.5 us (2%)
    psum x1, waiting for transfers between devices, body(): weight_total = lax.psum(weight_term, ('row', 'col'))  246 us
    reduce_scatter x1, waiting for transfers between devices, body(): lax.psum_scatter(partial_rows, 'col', scatter_dimension=0, tiled=True)  101 us
    scatter-add x3, other arithmetic, forward_group(): jax.ops.segment_sum(product, coords_part[:, 0], num_segments=block_rows /...  57.5 us
    all_gather x1, waiting for transfers between devices, body(): grad_rows = lax.all_gather(grad_total, 'col', axis=0, tiled=True)  45 us
    reduce_scatter x1, waiting for transfers between devices, body(): lax.psum_scatter(partial_cols, 'row', scatter_dimension=0, tiled=True)  42.6 us
    scatter-add x3, other arithmetic, backward_group(): jax.ops.segment_sum(product, coords_part[:, 1], num_segments=block_cols /...  37.1 us
    all_gather x1, blocking collectives, body(): panel = lax.all_gather(mixed, 'row', axis=0, tiled=True)  30.2 us
    dot_general x3, matrix products, forward_group(): jnp.einsum('tij,tjh->tih', tiles_part, picked, preferred_element_type=jnp...  21.9 us
  transfers between devices with their start and end apart: 4, of which 4 were waited for; matrix products, arithmetic and copies ran while one was open for 2% of the time, Pallas kernels for 0%

commit v1 on v0

--- a/solution.py
+++ b/solution.py
@@ -76,7 +76,8 @@
         jnp.bfloat16
     )
     weight_term = jnp.dot(features.T, grad_projected, preferred_element_type=jnp.float32)
-    weight_total = lax.psum(weight_term, ("row", "col"))
+    partial = lax.psum(weight_term, "col")
+    weight_total = lax.psum(partial, "row")
     scale_factor = 1.0 / math.sqrt(node_count * rows_size * cols_size)
     grad_weight = weight_total * jnp.float32(scale_factor)
     return (output, grad_features, grad_weight)

time: 662 us -> 755 us (1.14)
  waiting for transfers between devices: 435 us -> 527 us
    psum x1 -> x2, waiting for transfers between devices: 246 us -> 339 us  [the longest x1 256 us: body(): partial = lax.psum(weight_term, 'col')]
  transfers between devices with their start and end apart: 4 -> 5, of which waited for: 4 -> 5; matrix products, arithmetic and copies ran while one was open for 2% -> 1% of each run, Pallas kernels for 0% -> 0%
where the time goes in v1:
time: 755 us; the launch traced here: 754 us
  waiting for transfers between devices  527 us (70%)
  other arithmetic  98 us (13%)
  matrix products  48.4 us (6%)
  local copies, waits for them, and re-layouts  35.1 us (5%)
  blocking collectives  30.2 us (4%)
  between operations  14.5 us (2%)
    psum x1, waiting for transfers between devices, body(): partial = lax.psum(weight_term, 'col')  256 us
    reduce_scatter x1, waiting for transfers between devices, body(): lax.psum_scatter(partial_rows, 'col', scatter_dimension=0, tiled=True)  101 us
    psum x1, waiting for transfers between devices, body(): weight_total = lax.psum(partial, 'row')  82.7 us
    scatter-add x3, other arithmetic, forward_group(): jax.ops.segment_sum(product, coords_part[:, 0], num_segments=block_rows /...  57.5 us
    all_gather x1, waiting for transfers between devices, body(): grad_rows = lax.all_gather(grad_total, 'col', axis=0, tiled=True)  45 us
    reduce_scatter x1, waiting for transfers between devices, body(): lax.psum_scatter(partial_cols, 'row', scatter_dimension=0, tiled=True)  42.6 us
    scatter-add x3, other arithmetic, backward_group(): jax.ops.segment_sum(product, coords_part[:, 1], num_segments=block_cols /...  37.1 us
    all_gather x1, blocking collectives, body(): panel = lax.all_gather(mixed, 'row', axis=0, tiled=True)  30.2 us
  transfers between devices with their start and end apart: 5, of which 5 were waited for; matrix products, arithmetic and copies ran while one was open for 1% of the time, Pallas kernels for 0%

profile of v1, /device:TPU:2, one launch (start us, length us, event | category | flops | bytes accessed | tf_op | source)
XLA Modules:
  0.0 754.0 jit_solution(8574432269257557413)
XLA Ops:
  7.2 0.0 reduce-scatter.3.cloned.1.call-start
  7.2 0.8 reshape_reshape.8
  8.7 0.7 broadcast_compare_fusion
  9.3 1.0 fusion.10
  10.3 30.2 %all_gather.6 = bf16[1024,256]{1,0:T(8,128)(2,1)S(1)} all-gather(bf16[128,256]{1,0:T(8,128)(2,1)S(1)} %fusion.10), channel_id=1, replica_groups=mesh['row'=8,'col'=32] {'row'}, dimensions={0}, use_global_device_ids=true | all-gather | bytes 589824 | tf_op jit(solution)/shard_map/all_gather | solution.py:39
  40.5 2.4 broadcast.43
  42.9 87.8 %while.20 = (s32[]{:T(128)}, f32[32,128,256]{2,1,0:T(8,128)}, s32[3,64,2]{1,2,0:T(2,128)S(1)}, bf16[3,64,128,128]{3,2,1,0:T(8,128)(2,1)}, bf16[8,128,256]{2,1,0:...) while((s32[]{:T(128)}, f32[32,128,256]{2,1,0:T(8,128)}, s32[3,64,2]{1,2,0:T(2,128)S(1)}, ...), condition=%wide.region_2.3_spmd, body=%wide.region_0.2_spmd.sunk | while | flops 541066432 | bytes 48242772 | solution.py:22
  43.0 2.8 gather_fusion
  45.7 7.3 broadcast_multiply_fusion.5
  53.0 19.1 %scatter_fusion = f32[32,128,256]{2,1,0:T(8,128)} fusion(f32[32,128,256]{2,1,0:T(8,128)} %get-tuple-element.213, s32[64]{0:T(128)S(1)} %get-tuple-element.195, f32[64,128,256]{2,1,0:T(8,128)} %broadcast_multiply_fusion.5), kind=kCustom, calls=%fused_computation.2.clone.1 | custom fusion | flops 2097152 | bytes 25166080 | tf_op jit(solution)/shard_map/while/body/eval_jaxpr/scatter-add | solution.py:46
  72.2 2.8 gather_fusion
  75.0 7.3 broadcast_multiply_fusion.5
  82.3 19.3 %scatter_fusion = f32[32,128,256]{2,1,0:T(8,128)} fusion(f32[32,128,256]{2,1,0:T(8,128)} %get-tuple-element.213, s32[64]{0:T(128)S(1)} %get-tuple-element.195, f32[64,128,256]{2,1,0:T(8,128)} %broadcast_multiply_fusion.5), kind=kCustom, calls=%fused_computation.2.clone.1 | custom fusion | flops 2097152 | bytes 25166080 | tf_op jit(solution)/shard_map/while/body/eval_jaxpr/scatter-add | solution.py:46
  101.6 2.8 gather_fusion
  104.3 7.3 broadcast_multiply_fusion.5
  111.6 19.1 %scatter_fusion = f32[32,128,256]{2,1,0:T(8,128)} fusion(f32[32,128,256]{2,1,0:T(8,128)} %get-tuple-element.213, s32[64]{0:T(128)S(1)} %get-tuple-element.195, f32[64,128,256]{2,1,0:T(8,128)} %broadcast_multiply_fusion.5), kind=kCustom, calls=%fused_computation.2.clone.1 | custom fusion | flops 2097152 | bytes 25166080 | tf_op jit(solution)/shard_map/while/body/eval_jaxpr/scatter-add | solution.py:46
  130.8 0.0 reduce-scatter.3.cloned.1.call-update
  130.8 0.0 all-gather.2.cloned.1.call-start
  130.9 101.0 %reduce-scatter.3.cloned.1.call-done = f32[128,256]{1,0:T(8,128)} async-done(((f32[4096,256]{1,0:T(8,128)}), f32[128,256]{1,0:T(8,128)}) %reduce-scatter.3.cloned.1.call-update) | async-done | bytes 131088 | tf_op jit(solution)/shard_map/reduce_scatter | solution.py:54
  231.8 1.7 fusion.13
  233.5 0.0 all-gather.2.cloned.1.call-update
  233.5 0.0 reduce-scatter.5.cloned.1.call-start
  233.6 8.6 %copy.14 = bf16[1,1,192,128,128]{3,4,2,1,0:T(8,128)(2,1)} copy(bf16[1,1,192,128,128]{4,3,2,1,0:T(8,128)(2,1)} %bitcast.65) | data formatting | bytes 12582912 | tf_op args[4]
  242.1 45.0 %all-gather.2.cloned.1.call-done = bf16[4096,256]{1,0:T(8,128)(2,1)} async-done(((bf16[128,256]{1,0:T(8,128)(2,1)}), bf16[4096,256]{1,0:T(8,128)(2,1)}) %all-gather.2.cloned.1.call-update) | async-done | bytes 2097168 | tf_op jit(solution)/shard_map/all_gather | solution.py:58
  287.2 0.1 broadcast.48
  287.3 72.3 %while.21 = (s32[]{:T(128)}, f32[8,128,256]{2,1,0:T(8,128)S(1)}, s32[3,64,2]{1,2,0:T(2,128)S(1)}, bf16[3,64,128,128]{2,3,1,0:T(8,128)(2,1)}, bf16[32,128,256]{2,...) while((s32[]{:T(128)}, f32[8,128,256]{2,1,0:T(8,128)S(1)}, s32[3,64,2]{1,2,0:T(2,128)S(1)}, ...), condition=%wide.region_6.7_spmd, body=%wide.region_4.6_spmd.sunk | while | flops 541066432 | bytes 48242772 | solution.py:22
  287.3 4.4 gather_fusion.1
  291.7 7.3 broadcast_multiply_fusion.6
  299.0 12.4 %scatter_fusion.1 = f32[8,128,256]{2,1,0:T(8,128)S(1)} fusion(f32[8,128,256]{2,1,0:T(8,128)S(1)} %get-tuple-element.234, s32[64]{0:T(128)S(1)} %get-tuple-element.203, f32[64,128,256]{2,1,0:T(8,128)} %broadcast_multiply_fusion.6), kind=kCustom, calls=%fused_computation.3.clone.1 | custom fusion | flops 2097152 | bytes 25166080 | tf_op jit(solution)/shard_map/while/body/eval_jaxpr/scatter-add | solution.py:65
  311.5 4.4 gather_fusion.1
  315.8 7.3 broadcast_multiply_fusion.6
  323.1 12.4 %scatter_fusion.1 = f32[8,128,256]{2,1,0:T(8,128)S(1)} fusion(f32[8,128,256]{2,1,0:T(8,128)S(1)} %get-tuple-element.234, s32[64]{0:T(128)S(1)} %get-tuple-element.203, f32[64,128,256]{2,1,0:T(8,128)} %broadcast_multiply_fusion.6), kind=kCustom, calls=%fused_computation.3.clone.1 | custom fusion | flops 2097152 | bytes 25166080 | tf_op jit(solution)/shard_map/while/body/eval_jaxpr/scatter-add | solution.py:65
  335.6 4.4 gather_fusion.1
  339.9 7.3 broadcast_multiply_fusion.6
  347.2 12.4 %scatter_fusion.1 = f32[8,128,256]{2,1,0:T(8,128)S(1)} fusion(f32[8,128,256]{2,1,0:T(8,128)S(1)} %get-tuple-element.234, s32[64]{0:T(128)S(1)} %get-tuple-element.203, f32[64,128,256]{2,1,0:T(8,128)} %broadcast_multiply_fusion.6), kind=kCustom, calls=%fused_computation.3.clone.1 | custom fusion | flops 2097152 | bytes 25166080 | tf_op jit(solution)/shard_map/while/body/eval_jaxpr/scatter-add | solution.py:65
  359.6 1.0 copy-done.1
  360.6 0.0 reduce-scatter.5.cloned.1.call-update
  360.6 0.0 all-reduce.3.cloned.1.call-start
  360.7 42.6 %reduce-scatter.5.cloned.1.call-done = f32[128,256]{1,0:T(8,128)} async-done(((f32[1024,256]{1,0:T(8,128)}), f32[128,256]{1,0:T(8,128)}) %reduce-scatter.5.cloned.1.call-update) | async-done | bytes 131088 | tf_op jit(solution)/shard_map/reduce_scatter | solution.py:73
  403.3 1.8 convolution_bitcast_fusion
  405.1 0.0 all-reduce.3.cloned.1.call-update
  405.1 0.0 all-reduce.5.cloned.1.call-start
  405.2 256.1 %all-reduce.3.cloned.1.call-done = f32[128,256]{0,1:T(8,128)} async-done(((f32[128,256]{0,1:T(8,128)}), f32[128,256]{0,1:T(8,128)}) %all-reduce.3.cloned.1.call-update) | async-done | bytes 131088 | tf_op jit(solution)/shard_map/psum | solution.py:79
  661.3 0.0 all-reduce.5.cloned.1.call-update
  661.3 1.7 convolution_convert_fusion.1
  663.1 82.7 %all-reduce.5.cloned.1.call-done = f32[128,256]{0,1:T(8,128)} async-done(((f32[128,256]{0,1:T(8,128)}), f32[128,256]{0,1:T(8,128)}) %all-reduce.5.cloned.1.call-update) | async-done | bytes 131088 | tf_op jit(solution)/shard_map/psum | solution.py:80
  745.8 0.9 broadcast_multiply_fusion.2
  746.7 0.8 copy.18
  (36 shorter events, 0.2 us)
Async XLA Ops:
  7.2 2.2 copy-start
  7.2 224.6 %reduce-scatter.3.cloned.1.call-start = ((), (), s32[]{:S(2)}) async-start(), calls=%async_computation.2 | async-start | bytes 4325376 | tf_op jit(solution)/shard_map/reduce_scatter | solution.py:54
  130.8 101.0 %copy-start.3 = (bf16[128,256]{1,0:T(8,128)(2,1)S(1)}, bf16[128,256]{1,0:T(8,128)(2,1)}, u32[]{:S(2)}) copy-start(bf16[128,256]{1,0:T(8,128)(2,1)} %param.19) | copy-start | bytes 196612
  130.8 156.4 %all-gather.2.cloned.1.call-start = ((), (), s32[]{:S(2)}) async-start(), calls=%async_computation.3 | async-start | bytes 2162688 | tf_op jit(solution)/shard_map/all_gather | solution.py:58
  233.5 169.8 %reduce-scatter.5.cloned.1.call-start = ((), (), s32[]{:S(2)}) async-start(), calls=%async_computation.4 | async-start | bytes 1179648 | tf_op jit(solution)/shard_map/reduce_scatter | solution.py:73
  287.3 73.4 %copy-start.4 = (s32[128]{0:T(128)S(1)}, s32[128]{0:T(128)}, u32[]{:S(2)}) copy-start(s32[128]{0:T(128)} %param.15) | copy-start | bytes 1540
  287.3 116.0 %copy-start.2 = (bf16[128,128]{1,0:T(8,128)(2,1)S(1)}, bf16[128,128]{1,0:T(8,128)(2,1)}, u32[]{:S(2)}) copy-start(bf16[128,128]{1,0:T(8,128)(2,1)} %param.12) | copy-start | bytes 98308
  359.6 1.0 copy-start.1
  360.6 300.7 %all-reduce.3.cloned.1.call-start = ((), (), s32[]{:S(2)}) async-start(), calls=%async_computation.5 | async-start | bytes 262144 | tf_op jit(solution)/shard_map/psum | solution.py:79
  405.1 340.6 %all-reduce.5.cloned.1.call-start = ((), (), s32[]{:S(2)}) async-start(), calls=%async_computation.6 | async-start | bytes 262144 | tf_op jit(solution)/shard_map/psum | solution.py:80
Sparse Core Ops, SparseCore 0:
  130.9 100.8 reduce-scatter.2
  235.0 52.1 all-gather.1
  360.7 42.4 reduce-scatter.4
  406.3 254.9 all-reduce.2
  663.8 81.9 all-reduce.4
